TPU v7x, 256 devices: a whole 4x4x8 slice. The times are simulated.
256 devices in a mesh: req: 32 (over y, z), head: 8 (over x, core).
Axes of the slice: x: 4, y: 4, z: 8, core: 2. Of those that a mesh axis runs over, the one named last changes fastest.
Arguments:
- tokens: bfloat16 [256, 1024], P('req'), may hold values from -6 to 6
- lengths: int32 [256], P('req'), may hold values from 1 to 512, as said below
- slot_owner: int32 [256], P('req'), may hold values from 0 to 255, as said below
- positions: int32 [256], P('req'), may hold values from 0 to 8191
- variates: int32 [256], P('req'), may hold values from 0 to 7
- cache_variates: int32 [256, 512], P('req'), may hold values from 0 to 7
- kv_cache: bfloat16 [2, 2, 256, 512, 1024], P(None, None, 'req', None, 'head'), may hold values from -6 to 6
- attn_gain: float32 [2, 1024], replicated, may hold values from 0.1 to 1.9
- ffn_gain: float32 [2, 1024], replicated, may hold values from 0.1 to 1.9
- qkv_weight: bfloat16 [2, 1024, 3072], P(None, None, 'head'), may hold values from -0.1875 to 0.1875
- out_weight: bfloat16 [2, 1024, 1024], P(None, 'head'), may hold values from -0.1875 to 0.1875
- gate_up_weight: bfloat16 [2, 2, 1024, 4096], P(None, None, None, 'head'), may hold values from -0.1875 to 0.1875
- down_weight: bfloat16 [2, 4096, 1024], P(None, 'head'), may hold values from -0.09375 to 0.09375
- variate_bias: float32 [2, 2, 16], P(None, None, 'head'), may hold values from -2 to 300
Outputs:
- next_states: bfloat16 [256, 1024], P(('req', 'head'))
Inputs may be any that keep to these rules, and one draw needn't show every extreme that they name: `lengths`: live cache positions of each request; the largest is exactly 512 in every draw. `slot_owner`: each request is held in exactly one slot; taken in an order of non-increasing length, the requests fill slot t of every req index in turn t = 0, 1, ..., the req indices in rising order on even turns and in falling order on odd ones; no two slots of one req index hold requests of the same device of next_states (the same 1 request).
All inputs are finite; a program needn't handle non-finite values.
Results may differ from a plain program's by a relative error of at most 0.02.
Values may be sent and summed in bfloat16 or wider, within the bound.
A program may use at most 64 MiB of HBM per device.

v0:
```python
import jax
import jax.numpy as jnp
from jax import lax
from jax.sharding import PartitionSpec as P

HD = 64
LAYERS = 2
neg_fill = -1e30


def rms_scale(stream, gain_row):
    return stream * lax.rsqrt(jnp.mean(stream * stream, axis=-1, keepdims=True) + 1e-06) * gain_row


def rotary(vectors, time_ids):
    half_width = vectors.shape[-1] // 2
    frequency = 10000.0 ** (-2.0 * jnp.arange(half_width, dtype=jnp.float32) / vectors.shape[-1])
    angles = time_ids.astype(jnp.float32)[:, None, None] * frequency[None, None, :]
    cosine = jnp.cos(angles)
    sine_part = jnp.sin(angles)
    front_half = vectors[..., :half_width]
    back_half = vectors[..., half_width:]
    return jnp.concatenate(
        [front_half * cosine - back_half * sine_part, front_half * sine_part + back_half * cosine],
        axis=-1,
    )


def attend(
    queries,
    key_new,
    value_new,
    cached_keys,
    cached_values,
    cache_var,
    cache_lengths,
    variate_ids,
    same_bias,
    diff_bias,
):
    row_count, cache_len, width = cached_keys.shape
    local_heads = queries.shape[1]
    score_scale = HD ** (-0.5)
    diagonal_mask = jnp.eye(local_heads, dtype=jnp.bfloat16)
    q_block = (queries[:, :, :, None] * diagonal_mask[None, :, None, :]).reshape(
        row_count, local_heads * HD, local_heads
    )
    raw_scores = jnp.einsum(
        "rcf,rfh->rch", cached_keys, q_block, preferred_element_type=jnp.float32
    )
    score_bias = jnp.where(
        (cache_var == variate_ids[:, None])[:, :, None],
        same_bias[None, None, :],
        diff_bias[None, None, :],
    )
    scores = raw_scores * score_scale + score_bias
    live_mask = jnp.arange(cache_len, dtype=jnp.int32)[None, :] < cache_lengths[:, None]
    scores = jnp.where(live_mask[:, :, None], scores, neg_fill)
    self_score = (
        jnp.sum(queries.astype(jnp.float32) * key_new.astype(jnp.float32), axis=-1) * score_scale
        + same_bias[None, :]
    )
    row_top = jnp.maximum(jnp.max(scores, axis=1), self_score)
    weights = jnp.exp(scores - row_top[:, None, :])
    self_weight = jnp.exp(self_score - row_top)
    denominator = jnp.sum(weights, axis=1) + self_weight
    probs_bf16 = (weights / denominator[:, None, :]).astype(jnp.bfloat16)
    self_prob = (self_weight / denominator).astype(jnp.bfloat16)
    mixed_full = jnp.einsum(
        "rch,rcf->rhf", probs_bf16, cached_values, preferred_element_type=jnp.float32
    )
    mask_float = diagonal_mask.astype(jnp.float32)
    mixed_heads = jnp.sum(
        mixed_full.reshape(row_count, local_heads, local_heads, HD) * mask_float[None, :, :, None],
        axis=2,
    )
    mixed_heads = mixed_heads + self_prob.astype(jnp.float32)[:, :, None] * value_new.astype(
        jnp.float32
    )
    return mixed_heads.reshape(row_count, local_heads * HD).astype(jnp.bfloat16)


def per_device(
    tokens,
    lengths,
    slot_owner,
    positions,
    variates,
    cache_variates,
    kv_cache,
    attn_gain,
    ffn_gain,
    qkv_weight,
    out_weight,
    gate_up_weight,
    down_weight,
    variate_bias,
):
    head_count = lax.axis_size("head")
    head_place = lax.axis_index("head")
    slot_count = slot_owner.shape[0]
    token_share = slot_count // head_count
    all_lengths, all_times, all_variates, all_owners = (
        lax.all_gather(lengths, "req", axis=0, tiled=True),
        lax.all_gather(positions, "req", axis=0, tiled=True),
        lax.all_gather(variates, "req", axis=0, tiled=True),
        lax.all_gather(slot_owner, "req", axis=0, tiled=True),
    )
    all_tokens = lax.all_gather(tokens, "req", axis=0, tiled=True)
    slot_tokens = jnp.take(all_tokens, slot_owner, axis=0).astype(jnp.float32)
    cache_lengths = jnp.take(all_lengths, slot_owner)
    time_ids = jnp.take(all_times, slot_owner)
    variate_ids = jnp.take(all_variates, slot_owner)
    residual = lax.dynamic_slice_in_dim(slot_tokens, head_place * token_share, token_share, 0)
    local_heads = kv_cache.shape[-1] // HD
    for layer_index in range(LAYERS):
        if layer_index == 0:
            normed = rms_scale(slot_tokens, attn_gain[0]).astype(jnp.bfloat16)
        else:
            normed = lax.all_gather(
                rms_scale(residual, attn_gain[layer_index]).astype(jnp.bfloat16),
                "head",
                axis=0,
                tiled=True,
            )
        projected = jnp.dot(normed, qkv_weight[layer_index], preferred_element_type=jnp.float32)
        projected = projected.reshape(slot_count, local_heads, 3, HD)
        queries = rotary(projected[:, :, 0], time_ids).astype(jnp.bfloat16)
        key_new = rotary(projected[:, :, 1], time_ids).astype(jnp.bfloat16)
        value_new = projected[:, :, 2].astype(jnp.bfloat16)
        attended = attend(
            queries,
            key_new,
            value_new,
            kv_cache[layer_index, 0],
            kv_cache[layer_index, 1],
            cache_variates,
            cache_lengths,
            variate_ids,
            variate_bias[layer_index, 0],
            variate_bias[layer_index, 1],
        )
        out_partial = jnp.dot(attended, out_weight[layer_index], preferred_element_type=jnp.float32)
        residual = residual + lax.psum_scatter(
            out_partial.astype(jnp.bfloat16), "head", scatter_dimension=0, tiled=True
        ).astype(jnp.float32)
        ffn_input = lax.all_gather(
            rms_scale(residual, ffn_gain[layer_index]).astype(jnp.bfloat16),
            "head",
            axis=0,
            tiled=True,
        )
        paired = jnp.einsum(
            "rd,gdf->grf",
            ffn_input,
            gate_up_weight[layer_index],
            preferred_element_type=jnp.float32,
        )
        hidden = (jax.nn.silu(paired[0]) * paired[1]).astype(jnp.bfloat16)
        ffn_partial = jnp.dot(hidden, down_weight[layer_index], preferred_element_type=jnp.float32)
        residual = residual + lax.psum_scatter(
            ffn_partial.astype(jnp.bfloat16), "head", scatter_dimension=0, tiled=True
        ).astype(jnp.float32)
    final_rows = residual.astype(jnp.bfloat16)
    own_place = lax.axis_index("req") * head_count + head_place
    request_ids = own_place * token_share + jnp.arange(token_share, dtype=jnp.int32)
    matches = all_owners[None, :] == request_ids[:, None]
    slot_index = jnp.sum(
        jnp.where(matches, jnp.arange(all_owners.shape[0], dtype=jnp.int32)[None, :], 0), axis=1
    )
    everything = lax.all_gather(final_rows, ("req", "head"), axis=0, tiled=True)
    return jnp.take(everything, slot_index, axis=0)


def solution(mesh):
    return jax.shard_map(
        per_device,
        mesh=mesh,
        in_specs=(
            P("req", None),
            P("req"),
            P("req"),
            P("req"),
            P("req"),
            P("req", None),
            P(None, None, "req", None, "head"),
            P(),
            P(),
            P(None, None, "head"),
            P(None, "head", None),
            P(None, None, None, "head"),
            P(None, "head", None),
            P(None, None, "head"),
        ),
        out_specs=P(("req", "head"), None),
        check_vma=False,
    )
```

profile of v0, /device:TPU:1, one launch (start us, length us, event | category | flops | bytes accessed | tf_op | source)
XLA Modules:
  0.0 306.1 jit_solution(2157831063779013560)
XLA Ops:
  0.0 1.3 dynamic-slice.4
  2.0 0.9 dynamic-update-slice.1
  2.8 0.8 dynamic-update-slice.4
  3.7 0.8 dynamic-update-slice.2
  4.5 0.8 dynamic-update-slice.3
  5.3 20.3 %all-reduce.8 = (s32[256]{0:T(256)S(1)}, s32[256]{0:T(256)S(1)}, s32[256]{0:T(256)S(1)}, s32[256]{0:T(256)S(1)}) all-reduce(s32[256]{0:T(256)S(1)} %dynamic-update-slice.1, s32[256]{0:T(256)S(1)} %dynamic-update-slice.4, s32[256]{0:T(256)S(1)} %dynamic-update-slice.2, s32[256]{0:T(256)S(1)} %dynamic-update-slice.3), channel_id=1, replica_groups=mesh['req'=32,'head'=8] {'req'}, use_global_device_ids=true, to_apply=%add | all-reduce | flops 1024 | bytes 8192
  25.6 0.6 fusion.84
  28.2 0.8 slice_bitcast_fusion.7
  28.9 0.7 compare_select_fusion
  29.6 0.6 gather_fusion.2
  30.3 0.7 select_convert_fusion
  30.9 0.6 gather_fusion.1
  31.6 0.6 gather_fusion.3
  32.2 0.8 iota_compare_fusion
  33.0 0.1 copy.70
  33.2 0.1 mul.378
  33.3 1.6 slice_bitcast_fusion
  34.9 0.3 copy.67
  35.2 35.6 %all_gather.28 = bf16[256,1024]{1,0:T(8,128)(2,1)S(1)} all-gather(bf16[8,1024]{1,0:T(8,128)(2,1)S(1)} %copy-done.2), channel_id=1, replica_groups=mesh['req'=32,'head'=8] {'req'}, dimensions={0}, use_global_device_ids=true | all-gather | bytes 540672 | tf_op jit(solution)/shard_map/all_gather | solution.py:109
  70.8 0.6 gather_fusion
  71.4 0.2 multiply_reduce_fusion
  71.6 0.4 fusion.39
  72.1 0.1 multiply_cosine_fusion
  72.4 0.1 convert_element_type.227
  72.4 1.7 fusion.94
  74.1 0.2 multiply_reduce_fusion.4
  74.3 0.1 copy.71
  74.4 0.2 fusion.36
  74.6 1.5 fusion.23
  76.1 0.1 reshape.405
  76.2 0.1 multiply_reduce_fusion.2
  76.5 0.1 convert_element_type.238
  76.6 0.1 convolution_convert_fusion.3
  76.7 36.7 %all-reduce.4 = bf16[8,1024]{1,0:T(8,128)(2,1)S(1)} all-reduce(bf16[8,1024]{1,0:T(8,128)(2,1)S(1)} %convolution_convert_fusion.3), channel_id=2, replica_groups=mesh['req'=32,'head'=8] {'head'}, use_global_device_ids=true, to_apply=%region_6.8.clone | all-reduce | flops 8192 | bytes 32768
  113.4 0.6 dynamic-slice.9
  114.1 1.3 multiply_reduce_fusion.7
  116.1 16.3 %all-gather = bf16[8,1,1024]{2,1,0:T(2,128)(2,1)S(1)} all-gather(bf16[1,1,1024]{2,1,0:T(2,128)(2,1)S(1)} %convert_bitcast_fusion.2), channel_id=1, replica_groups=mesh['req'=32,'head'=8] {'head'}, dimensions={0}, use_global_device_ids=true | all-gather | bytes 18432 | tf_op jit(solution)/shard_map/all_gather | solution.py:147
  132.4 2.0 fusion.6
  134.3 1.5 convolution_convert_fusion.2
  135.8 20.4 %all-reduce.5 = bf16[8,1024]{1,0:T(8,128)(2,1)S(1)} all-reduce(bf16[8,1024]{1,0:T(8,128)(2,1)S(1)} %convolution_convert_fusion.2), channel_id=3, replica_groups=mesh['req'=32,'head'=8] {'head'}, use_global_device_ids=true, to_apply=%region_8.10.clone | all-reduce | flops 8192 | bytes 32768
  156.2 1.3 multiply_reduce_fusion.6
  157.5 0.3 copy.75
  158.5 16.3 %all-gather.1 = bf16[8,1,1024]{2,1,0:T(2,128)(2,1)S(1)} all-gather(bf16[1,1,1024]{2,1,0:T(2,128)(2,1)S(1)} %convert_bitcast_fusion.1), channel_id=1, replica_groups=mesh['req'=32,'head'=8] {'head'}, dimensions={0}, use_global_device_ids=true | all-gather | bytes 18432 | tf_op jit(solution)/shard_map/all_gather | solution.py:120
  174.8 0.4 fusion.43
  175.2 0.1 subtract_convert_fusion
  175.4 0.1 convert_element_type.247
  175.4 1.8 fusion.95
  177.3 0.2 multiply_reduce_fusion.3
  177.4 0.1 copy.79
  177.5 0.2 fusion.37
  177.7 1.5 fusion.19
  179.3 0.1 reshape.406
  179.4 0.1 multiply_reduce_fusion.1
  179.6 0.1 convert_element_type.256
  179.7 0.1 convolution_convert_fusion.1
  179.9 20.4 %all-reduce.6 = bf16[8,1024]{1,0:T(8,128)(2,1)S(1)} all-reduce(bf16[8,1024]{1,0:T(8,128)(2,1)S(1)} %convolution_convert_fusion.1), channel_id=4, replica_groups=mesh['req'=32,'head'=8] {'head'}, use_global_device_ids=true, to_apply=%region_14.16.clone | all-reduce | flops 8192 | bytes 32768
  200.3 1.3 multiply_reduce_fusion.5
  202.2 16.3 %all-gather.2 = bf16[8,1,1024]{2,1,0:T(2,128)(2,1)S(1)} all-gather(bf16[1,1,1024]{2,1,0:T(2,128)(2,1)S(1)} %convert_bitcast_fusion), channel_id=1, replica_groups=mesh['req'=32,'head'=8] {'head'}, dimensions={0}, use_global_device_ids=true | all-gather | bytes 18432 | tf_op jit(solution)/shard_map/all_gather | solution.py:147
  218.5 2.0 fusion.9
  220.5 0.3 convolution_convert_fusion
  220.7 20.4 %all-reduce.7 = bf16[8,1024]{1,0:T(8,128)(2,1)S(1)} all-reduce(bf16[8,1024]{1,0:T(8,128)(2,1)S(1)} %convolution_convert_fusion), channel_id=5, replica_groups=mesh['req'=32,'head'=8] {'head'}, use_global_device_ids=true, to_apply=%region_16.18.clone | all-reduce | flops 8192 | bytes 32768
  241.1 0.7 fusion.70
  241.8 63.7 %all-gather.3 = bf16[256,1,1024]{2,1,0:T(2,128)(2,1)S(1)} all-gather(bf16[1,1,1024]{2,1,0:T(2,128)(2,1)S(1)} %fusion.70), channel_id=1, replica_groups=mesh['req'=32,'head'=8] {'req','head'}, dimensions={0}, use_global_device_ids=true | all-gather | bytes 526336 | tf_op jit(solution)/shard_map/all_gather | solution.py:171
  305.5 0.6 fusion.65
  (46 shorter events, 0.9 us)
Async XLA Ops:
  0.0 71.6 %slice-start = ((f32[2,1024]{1,0:T(2,128)}), f32[1,1024]{1,0:T(1,128)S(1)}, s32[]{:S(2)}) async-start(f32[2,1024]{1,0:T(2,128)} %param.23), calls=%async_computation | async-start | bytes 8192 | tf_op jit(solution)/shard_map/slice | solution.py:118
  0.0 35.2 %copy-start.2 = (bf16[8,1024]{1,0:T(8,128)(2,1)S(1)}, bf16[8,1024]{1,0:T(8,128)(2,1)}, u32[]{:S(2)}) copy-start(bf16[8,1024]{1,0:T(8,128)(2,1)} %param.16) | copy-start | bytes 49156
  33.3 43.3 %copy-start = (bf16[2,128,1024]{2,1,0:T(8,128)(2,1)S(1)}, bf16[2,128,1024]{2,1,0:T(8,128)(2,1)}, u32[]{:S(2)}) copy-start(bf16[2,128,1024]{2,1,0:T(8,128)(2,1)} %param.26) | copy-start | bytes 1572868
  33.3 80.1 %copy-start.5 = (u32[256]{0:T(256)S(1)}, u32[256]{0:T(256)}, u32[]{:S(2)}) copy-start(u32[256]{0:T(256)} %constant.146) | copy-start | bytes 3076
  33.3 82.7 %copy-start.3 = (f32[2,1024]{1,0:T(2,128)S(1)}, f32[2,1024]{1,0:T(2,128)}, u32[]{:S(2)}) copy-start(f32[2,1024]{1,0:T(2,128)} %param.24) | copy-start | bytes 24580
  72.4 86.1 %copy-start.1 = (f32[2,1024]{1,0:T(2,128)S(1)}, f32[2,1024]{1,0:T(2,128)}, u32[]{:S(2)}) copy-start(f32[2,1024]{1,0:T(2,128)} %param.23) | copy-start | bytes 24580
  175.2 45.3 %copy-start.4 = (bf16[2,512,1024]{2,1,0:T(8,128)(2,1)S(1)}, bf16[2,512,1024]{2,1,0:T(8,128)(2,1)}, u32[]{:S(2)}) copy-start(bf16[2,512,1024]{2,1,0:T(8,128)(2,1)} %param.28) | copy-start | bytes 6291460
where the time goes:
time: 307 us; the launch traced here: 306 us
  blocking collectives  266 us (87%)
  matrix products  13.4 us (4%)
  local copies, waits for them, and re-layouts  11.9 us (4%)
  other arithmetic  9.74 us (3%)
  between operations  4.82 us (2%)
    unnamed x5, blocking collectives  118 us
    all_gather x1, blocking collectives, per_device(): everything = lax.all_gather(final_rows, ('req', 'head'), axis=0, tiled=True)  63.7 us
    all_gather x1, blocking collectives, per_device(): all_tokens = lax.all_gather(tokens, 'req', axis=0, tiled=True)  35.6 us
    all_gather x2, blocking collectives, per_device(): lax.all_gather(rms_scale(residual, ffn_gain[layer_index]).astype(jnp.bflo...  32.6 us
    all_gather x1, blocking collectives, per_device(): lax.all_gather(rms_scale(residual, attn_gain[layer_index]).astype(jnp.bfl...  16.3 us

commit v1 on v0

--- a/solution.py
+++ b/solution.py
@@ -106,7 +106,9 @@
         lax.all_gather(variates, "req", axis=0, tiled=True),
         lax.all_gather(slot_owner, "req", axis=0, tiled=True),
     )
-    all_tokens = lax.all_gather(tokens, "req", axis=0, tiled=True)
+    all_tokens = jnp.concatenate(
+        lax.all_to_all(jnp.stack([tokens] * lax.axis_size("req")), "req", 0, 0), axis=0
+    )
     slot_tokens = jnp.take(all_tokens, slot_owner, axis=0).astype(jnp.float32)
     cache_lengths = jnp.take(all_lengths, slot_owner)
     time_ids = jnp.take(all_times, slot_owner)

time: 307 us -> 271 us (0.88)
  blocking collectives: 266 us -> 216 us
  starting transfers between devices: 0 us -> 12.2 us
    all_gather x1 -> x0, blocking collectives: 35.6 us -> none  [per_device(): all_tokens = lax.all_gather(tokens, 'req', axis=0, tiled=True)]
    unnamed x5, blocking collectives: 118 us -> 104 us
    all_to_all x0 -> x1, starting transfers between devices: none -> 12.2 us  [per_device(): lax.all_to_all(jnp.stack([tokens] * lax.axis_size('req')), 'req', 0, 0)]
  transfers between devices with their start and end apart: 0 -> 1, of which waited for: 0 -> 0; matrix products, arithmetic and copies ran while one was open for 0% -> 4% of each run, Pallas kernels for 0% -> 0%
where the time goes in v1:
time: 271 us
  blocking collectives  216 us (80%)
  matrix products  14.4 us (5%)
  local copies, waits for them, and re-layouts  13.8 us (5%)
  starting transfers between devices  12.2 us (5%)
  other arithmetic  9.17 us (3%)
  between operations  5.08 us (2%)
    unnamed x5, blocking collectives  104 us
    all_gather x1, blocking collectives, per_device(): everything = lax.all_gather(final_rows, ('req', 'head'), axis=0, tiled=True)  62.7 us
    all_gather x2, blocking collectives, per_device(): lax.all_gather(rms_scale(residual, ffn_gain[layer_index]).astype(jnp.bflo...  32.6 us
    all_gather x1, blocking collectives, per_device(): lax.all_gather(rms_scale(residual, attn_gain[layer_index]).astype(jnp.bfl...  16.3 us
    all_to_all x1, starting transfers between devices, per_device(): lax.all_to_all(jnp.stack([tokens] * lax.axis_size('req')), 'req', 0, 0)  12.2 us
  transfers between devices with their start and end apart: 1, of which 0 were waited for; matrix products, arithmetic and copies ran while one was open for 4% of the time, Pallas kernels for 0%

profile of v1, /device:TPU:1, one launch (start us, length us, event | category | flops | bytes accessed | tf_op | source)
XLA Modules:
  0.0 270.5 jit_solution(6071292300538363986)
XLA Ops:
  0.0 1.6 stack.2
  1.6 12.2 %all-to-all-start = ((bf16[32,8,1024]{2,1,0:T(8,128)(2,1)}), bf16[32,8,1024]{2,1,0:T(8,128)(2,1)}, u32[]{:S(2)}, u32[]{:S(2)}) async-start(bf16[32,8,1024]{2,1,0:T(8,128)(2,1)} %stack.2), calls=%async_computation | async-start | bytes 1048576 | tf_op jit(solution)/shard_map/all_to_all | solution.py:110
  13.8 0.7 compare_select_fusion
  14.5 1.3 dynamic-slice.4
  16.4 0.9 dynamic-update-slice.1
  17.3 0.8 dynamic-update-slice.2
  18.1 0.8 dynamic-update-slice.3
  19.0 0.8 dynamic-update-slice.4
  19.8 19.1 %all-reduce.8 = (s32[256]{0:T(256)S(1)}, s32[256]{0:T(256)S(1)}, s32[256]{0:T(256)S(1)}, s32[256]{0:T(256)S(1)}) all-reduce(s32[256]{0:T(256)S(1)} %dynamic-update-slice.1, s32[256]{0:T(256)S(1)} %dynamic-update-slice.4, s32[256]{0:T(256)S(1)} %dynamic-update-slice.2, s32[256]{0:T(256)S(1)} %dynamic-update-slice.3), channel_id=1, replica_groups=mesh['req'=32,'head'=8] {'req'}, use_global_device_ids=true, to_apply=%add | all-reduce | flops 1024 | bytes 8192
  38.9 0.6 gather_fusion.2
  39.5 0.7 select_convert_fusion
  40.2 1.5 slice_bitcast_fusion
  41.7 0.6 fusion.84
  42.4 0.3 copy.67
  42.7 0.6 gather_fusion.1
  43.3 0.6 gather_fusion.3
  44.0 0.1 copy.70
  44.2 0.1 mul.378
  44.3 0.3 copy.75
  46.5 0.6 dynamic-slice.9
  47.2 0.1 multiply_cosine_fusion
  47.4 1.7 gather_fusion
  49.1 0.2 multiply_reduce_fusion
  49.3 0.4 fusion.39
  49.8 0.1 subtract_convert_fusion.2
  49.9 0.2 multiply_reduce_fusion.4
  50.0 0.1 copy.71
  50.2 0.1 convert_element_type.227
  50.3 1.7 fusion.94
  52.0 0.2 fusion.36
  52.2 1.5 fusion.23
  53.7 0.1 reshape.411
  53.9 0.1 multiply_reduce_fusion.2
  54.1 0.1 convert_element_type.238
  54.2 0.1 convolution_convert_fusion.3
  54.3 24.1 %all-reduce.4 = bf16[8,1024]{1,0:T(8,128)(2,1)S(1)} all-reduce(bf16[8,1024]{1,0:T(8,128)(2,1)S(1)} %convolution_convert_fusion.3), channel_id=2, replica_groups=mesh['req'=32,'head'=8] {'head'}, use_global_device_ids=true, to_apply=%region_6.8.clone | all-reduce | flops 8192 | bytes 32768
  78.4 1.3 multiply_reduce_fusion.7
  80.5 16.3 %all-gather = bf16[8,1,1024]{2,1,0:T(2,128)(2,1)S(1)} all-gather(bf16[1,1,1024]{2,1,0:T(2,128)(2,1)S(1)} %convert_bitcast_fusion.2), channel_id=1, replica_groups=mesh['req'=32,'head'=8] {'head'}, dimensions={0}, use_global_device_ids=true | all-gather | bytes 18432 | tf_op jit(solution)/shard_map/all_gather | solution.py:149
  96.8 2.0 fusion.6
  98.8 1.5 convolution_convert_fusion.2
  100.2 20.4 %all-reduce.5 = bf16[8,1024]{1,0:T(8,128)(2,1)S(1)} all-reduce(bf16[8,1024]{1,0:T(8,128)(2,1)S(1)} %convolution_convert_fusion.2), channel_id=3, replica_groups=mesh['req'=32,'head'=8] {'head'}, use_global_device_ids=true, to_apply=%region_8.10.clone | all-reduce | flops 8192 | bytes 32768
  120.6 1.3 multiply_reduce_fusion.6
  122.7 16.3 %all-gather.1 = bf16[8,1,1024]{2,1,0:T(2,128)(2,1)S(1)} all-gather(bf16[1,1,1024]{2,1,0:T(2,128)(2,1)S(1)} %convert_bitcast_fusion.1), channel_id=1, replica_groups=mesh['req'=32,'head'=8] {'head'}, dimensions={0}, use_global_device_ids=true | all-gather | bytes 18432 | tf_op jit(solution)/shard_map/all_gather | solution.py:122
  139.0 0.4 fusion.43
  139.4 0.1 subtract_convert_fusion
  139.5 0.2 multiply_reduce_fusion.3
  139.7 0.1 copy.79
  139.9 0.1 convert_element_type.247
  139.9 1.7 fusion.95
  141.6 0.2 fusion.37
  141.9 1.5 fusion.19
  143.4 0.1 reshape.412
  143.5 0.1 multiply_reduce_fusion.1
  143.8 0.1 convert_element_type.256
  143.8 0.1 convolution_convert_fusion.1
  144.0 20.4 %all-reduce.6 = bf16[8,1024]{1,0:T(8,128)(2,1)S(1)} all-reduce(bf16[8,1024]{1,0:T(8,128)(2,1)S(1)} %convolution_convert_fusion.1), channel_id=4, replica_groups=mesh['req'=32,'head'=8] {'head'}, use_global_device_ids=true, to_apply=%region_14.16.clone | all-reduce | flops 8192 | bytes 32768
  164.4 1.3 multiply_reduce_fusion.5
  166.5 16.3 %all-gather.2 = bf16[8,1,1024]{2,1,0:T(2,128)(2,1)S(1)} all-gather(bf16[1,1,1024]{2,1,0:T(2,128)(2,1)S(1)} %convert_bitcast_fusion), channel_id=1, replica_groups=mesh['req'=32,'head'=8] {'head'}, dimensions={0}, use_global_device_ids=true | all-gather | bytes 18432 | tf_op jit(solution)/shard_map/all_gather | solution.py:149
  182.8 2.0 fusion.9
  184.7 1.5 convolution_convert_fusion
  186.2 20.4 %all-reduce.7 = bf16[8,1024]{1,0:T(8,128)(2,1)S(1)} all-reduce(bf16[8,1024]{1,0:T(8,128)(2,1)S(1)} %convolution_convert_fusion), channel_id=5, replica_groups=mesh['req'=32,'head'=8] {'head'}, use_global_device_ids=true, to_apply=%region_16.18.clone | all-reduce | flops 8192 | bytes 32768
  206.6 0.7 fusion.70
  207.3 62.7 %all-gather.3 = bf16[256,1,1024]{2,1,0:T(2,128)(2,1)S(1)} all-gather(bf16[1,1,1024]{2,1,0:T(2,128)(2,1)S(1)} %fusion.70), channel_id=1, replica_groups=mesh['req'=32,'head'=8] {'req','head'}, dimensions={0}, use_global_device_ids=true | all-gather | bytes 526336 | tf_op jit(solution)/shard_map/all_gather | solution.py:173
  269.9 0.6 fusion.65
  (48 shorter events, 0.9 us)
Async XLA Ops:
  1.6 45.8 %all-to-all-start = ((bf16[32,8,1024]{2,1,0:T(8,128)(2,1)}), bf16[32,8,1024]{2,1,0:T(8,128)(2,1)}, u32[]{:S(2)}, u32[]{:S(2)}) async-start(bf16[32,8,1024]{2,1,0:T(8,128)(2,1)} %stack.2), calls=%async_computation | async-start | bytes 1048576 | tf_op jit(solution)/shard_map/all_to_all | solution.py:110
  13.7 32.8 %copy-start.5 = (u32[256]{0:T(256)S(1)}, u32[256]{0:T(256)}, u32[]{:S(2)}) copy-start(u32[256]{0:T(256)} %constant.146) | copy-start | bytes 3076
  13.8 33.4 %copy-start.4 = (f32[2,2,2]{2,1,0:T(2,128)S(1)}, f32[2,2,2]{2,1,0:T(2,128)}, u32[]{:S(2)}) copy-start(f32[2,2,2]{2,1,0:T(2,128)} %param.29) | copy-start | bytes 100
  13.8 33.5 %copy-start.2 = (s32[8,512]{1,0:T(8,128)S(1)}, s32[8,512]{1,0:T(8,128)}, u32[]{:S(2)}) copy-start(s32[8,512]{1,0:T(8,128)} %param.21) | copy-start | bytes 49156
  13.8 35.6 %slice-start = ((f32[2,1024]{1,0:T(2,128)}), f32[1,1024]{1,0:T(1,128)S(1)}, s32[]{:S(2)}) async-start(f32[2,1024]{1,0:T(2,128)} %param.23), calls=%async_computation.1 | async-start | bytes 8192 | tf_op jit(solution)/shard_map/slice | solution.py:120
  42.4 38.1 %copy-start.3 = (f32[2,1024]{1,0:T(2,128)S(1)}, f32[2,1024]{1,0:T(2,128)}, u32[]{:S(2)}) copy-start(f32[2,1024]{1,0:T(2,128)} %param.24) | copy-start | bytes 24580
  42.7 11.5 %copy-start = (bf16[2,128,1024]{2,1,0:T(8,128)(2,1)S(1)}, bf16[2,128,1024]{2,1,0:T(8,128)(2,1)}, u32[]{:S(2)}) copy-start(bf16[2,128,1024]{2,1,0:T(8,128)(2,1)} %param.26) | copy-start | bytes 1572868
  44.6 78.1 %copy-start.1 = (f32[2,1024]{1,0:T(2,128)S(1)}, f32[2,1024]{1,0:T(2,128)}, u32[]{:S(2)}) copy-start(f32[2,1024]{1,0:T(2,128)} %param.23) | copy-start | bytes 24580
